TPU v7x, 32 devices: a whole 2x2x4 slice. The times are simulated.
32 devices in a mesh: row: 8 (over z, core), col: 4 (over y, x).
Axes of the slice: x: 2, y: 2, z: 4, core: 2. Of those that a mesh axis runs over, the one named last changes fastest.
Arguments:
- running_cost: float32 [2048, 2048], P('row', 'col'), may hold values from 0.5 to 7.5, as said below
- control_x: float32 [2048, 2048], P('row', 'col'), may hold values from -6 to 6
- control_y: float32 [2048, 2048], P('row', 'col'), may hold values from -6 to 6
- prior_density: float32 [2048, 2048], P('row', 'col'), may hold values from 0.5 to 2
Outputs:
- value_field: float32 [2048, 2048], P('row', 'col')
- density: float32 [2048, 2048], P('row', 'col')
- ergodic: float32 [], replicated
Inputs may be any that keep to these rules, and one draw needn't show every extreme that they name: `running_cost`: strictly positive.
All inputs are finite; a program needn't handle non-finite values.
Results may differ from a plain program's by a relative error of at most 0.0003.
Values sent between devices are 32-bit elements; how exact they have to be, the bound alone decides.
No kernel may reach another device: no remote copies, remote signals or barrier semaphores. Data moves between devices by JAX's collectives and lax.ppermute only.
A program may use at most 64 MiB of HBM per device.

v0:
```python
import jax
import jax.numpy as jnp
from jax import lax
from jax.sharding import PartitionSpec as P

ITERS = 3
discount_rate = 0.05
diffusion = 0.25


def padded_2(cells, sides, width):
    for axis, dim in sides:
        count = lax.axis_size(axis)
        ends = count - 1
        head = lax.slice_in_dim(cells, 0, width, axis=dim)
        tail = lax.slice_in_dim(cells, cells.shape[dim] - width, cells.shape[dim], axis=dim)
        cells = jnp.concatenate(
            [
                lax.ppermute(tail, axis, [(i, (i + 1) % count) for i in range(ends)]),
                cells,
                lax.ppermute(head, axis, [((i + 1) % count, i) for i in range(ends)]),
            ],
            axis=dim,
        )
    return cells


def interior(padded):
    return padded[1:-1, 1:-1]


def neighbours(padded):
    return (padded[2:, 1:-1], padded[:-2, 1:-1], padded[1:-1, 2:], padded[1:-1, :-2])


def coefficients(conduct, padded_conduct, zeroth):
    weights = tuple(
        (diffusion * 0.5 * (conduct + outside) for outside in neighbours(padded_conduct))
    )
    center = zeroth + (weights[0] + weights[1] + (weights[2] + weights[3]))
    return (center,) + weights


def operator_apply(padded, coeffs):
    beside = neighbours(padded)
    inflow = (
        coeffs[1] * beside[0]
        + coeffs[2] * beside[1]
        + (coeffs[3] * beside[2] + coeffs[4] * beside[3])
    )
    return coeffs[0] * interior(padded) - inflow


def operate(source, coeffs):
    padded = padded_2(source, (("row", 0), ("col", 1)), 1)
    return (padded, operator_apply(padded, coeffs))


def products(residual, applied):
    return lax.psum((jnp.sum(residual * residual), jnp.sum(residual * applied)), ("row", "col"))


def conjugate(coeffs, forcing):
    solution = jnp.zeros_like(forcing)
    padded_solution = jnp.zeros((forcing.shape[0] + 2, forcing.shape[1] + 2), jnp.float32)
    residual = forcing
    padded_res, applied = operate(residual, coeffs)
    norm_now, product = products(residual, applied)
    step_size = norm_now / product
    direction, image_dir, padded_dir = (residual, applied, padded_res)
    for iteration in range(ITERS):
        solution = solution + step_size * direction
        if iteration + 1 < ITERS:
            residual = residual - step_size * image_dir
            padded_res, applied = operate(residual, coeffs)
            norm_next, product = products(residual, applied)
            beta_ratio = norm_next / norm_now
            step_size = norm_next / (product - beta_ratio * norm_next / step_size)
            direction = residual + beta_ratio * direction
            image_dir = applied + beta_ratio * image_dir
            norm_now = norm_next
    return (solution, padded_solution)


def body(running_cost, control_x, control_y, prior_density):
    control_cost = 0.5 * (control_x * control_x + control_y * control_y)
    conduct = 1.0 + control_cost
    forcing = running_cost + control_cost
    padded_conduct = padded_2(conduct, (("row", 0), ("col", 1)), 1)
    bellman = coefficients(conduct, padded_conduct, discount_rate)
    value_field, padded_solution = conjugate(bellman, forcing)
    padded_value = padded_2(value_field, (("row", 0), ("col", 1)), 1)
    beside = neighbours(padded_value)
    slope_row = 0.5 * (beside[0] - beside[1])
    slope_col = 0.5 * (beside[2] - beside[3])
    congestion = (slope_row * slope_row + slope_col * slope_col) / (2.0 * diffusion)
    planck = coefficients(conduct, padded_conduct, discount_rate + congestion)
    weighted = jnp.sum(prior_density * (forcing - discount_rate * value_field))
    weight_total = jnp.sum(prior_density)
    density, unused = conjugate(planck, prior_density)
    totals = lax.psum((weighted, weight_total), ("row", "col"))
    ergodic = totals[0] / totals[1]
    return (value_field, density, ergodic)


def solution(mesh):
    in_specs = (P("row", "col"), P("row", "col"), P("row", "col"), P("row", "col"))
    out_specs = (P("row", "col"), P("row", "col"), P())
    return jax.shard_map(body, mesh=mesh, in_specs=in_specs, out_specs=out_specs, check_vma=False)
```

profile of v0, /device:TPU:0, one launch (start us, length us, event | category | flops | bytes accessed | tf_op | source)
XLA Modules:
  0.0 410.6 jit_solution(13232752948674389063)
XLA Ops:
  0.6 1.5 broadcast_add_fusion
  2.2 2.4 collective-permute-start.5
  4.6 1.3 collective-permute-start.4
  5.9 5.2 %collective-permute-start.1 = (f32[1,512]{1,0:T(1,128)S(1)}, f32[1,512]{1,0:T(1,128)S(1)}, u32[]{:S(2)}, u32[]{:S(2)}) collective-permute-start(f32[1,512]{1,0:T(1,128)S(1)} %get-tuple-element.65), channel_id=1, source_target_pairs={{0,4},{4,8},{8,12},{12,16},{16,20},{20,24},{24,28},{1,5},{5,9},{9,... | collective-permute-start | bytes 6152 | tf_op jit(solution)/shard_map/ppermute | solution.py:19
  11.1 1.3 collective-permute-start
  12.5 1.3 collective-permute-start.6
  13.8 4.6 %collective-permute-start.7 = (f32[258,1]{1,0:T(8,128)S(1)}, f32[258,1]{1,0:T(8,128)S(1)}, u32[]{:S(2)}, u32[]{:S(2)}) collective-permute-start(f32[258,1]{1,0:T(8,128)S(1)} %get-tuple-element.52), channel_id=1, source_target_pairs={{0,1},{1,2},{2,3},{4,5},{5,6},{6,7},{8,9},{9,10},{10,11},{12,13},{... | collective-permute-start | bytes 3104 | tf_op jit(solution)/shard_map/ppermute | solution.py:19
  18.6 1.3 collective-permute-start.2
  19.9 4.9 %collective-permute-start.3 = (f32[258,1]{1,0:T(8,128)S(1)}, f32[258,1]{1,0:T(8,128)S(1)}, u32[]{:S(2)}, u32[]{:S(2)}) collective-permute-start(f32[258,1]{1,0:T(8,128)S(1)} %get-tuple-element.50), channel_id=1, source_target_pairs={{0,1},{1,2},{2,3},{4,5},{5,6},{6,7},{8,9},{9,10},{10,11},{12,13},{... | collective-permute-start | bytes 3104 | tf_op jit(solution)/shard_map/ppermute | solution.py:19
  24.8 2.5 collective-permute-done.2
  27.9 1.4 multiply_reduce_fusion.9
  29.3 44.4 %all-reduce.5 = (f32[]{:T(128)}, f32[]{:T(128)}) all-reduce(f32[]{:T(128)} %get-tuple-element.12, f32[]{:T(128)} %get-tuple-element.11), channel_id=1, replica_groups=mesh['row'=8,'col'=4] {'row','col'}, use_global_device_ids=true, to_apply=%region_1.0 | all-reduce | flops 2 | bytes 16 | tf_op jit(solution)/shard_map/psum | solution.py:60
  76.5 1.3 collective-permute-start.8
  77.8 3.4 collective-permute-done.8
  81.4 1.3 collective-permute-start.10
  82.7 4.8 %collective-permute-start.11 = (f32[258,1]{1,0:T(8,128)S(1)}, f32[258,1]{1,0:T(8,128)S(1)}, u32[]{:S(2)}, u32[]{:S(2)}) collective-permute-start(f32[258,1]{1,0:T(8,128)S(1)} %get-tuple-element.48), channel_id=1, source_target_pairs={{0,1},{1,2},{2,3},{4,5},{5,6},{6,7},{8,9},{9,10},{10,11},{12,13},{... | collective-permute-start | bytes 3104 | tf_op jit(solution)/shard_map/ppermute | solution.py:19
  88.5 1.5 collective-permute-done.11
  90.0 1.4 multiply_reduce_fusion.7
  91.4 44.4 %all-reduce.4 = (f32[]{:T(128)}, f32[]{:T(128)}) all-reduce(f32[]{:T(128)} %get-tuple-element.10, f32[]{:T(128)} %get-tuple-element.9), channel_id=1, replica_groups=mesh['row'=8,'col'=4] {'row','col'}, use_global_device_ids=true, to_apply=%region_5.0 | all-reduce | flops 2 | bytes 16 | tf_op jit(solution)/shard_map/psum | solution.py:60
  141.0 1.4 collective-permute-start.13
  142.4 1.3 collective-permute-start.12
  143.7 1.9 collective-permute-done.12
  145.7 1.3 collective-permute-start.14
  147.0 4.8 %collective-permute-start.15 = (f32[258,1]{1,0:T(8,128)S(1)}, f32[258,1]{1,0:T(8,128)S(1)}, u32[]{:S(2)}, u32[]{:S(2)}) collective-permute-start(f32[258,1]{1,0:T(8,128)S(1)} %get-tuple-element.46), channel_id=1, source_target_pairs={{0,1},{1,2},{2,3},{4,5},{5,6},{6,7},{8,9},{9,10},{10,11},{12,13},{... | collective-permute-start | bytes 3104 | tf_op jit(solution)/shard_map/ppermute | solution.py:19
  151.9 3.9 collective-permute-start.21
  155.8 1.3 collective-permute-start.20
  157.2 1.4 fusion.41
  158.6 41.7 %all-reduce.3 = (f32[]{:T(128)}, f32[]{:T(128)}) all-reduce(f32[]{:T(128)} %get-tuple-element.31, f32[]{:T(128)} %fusion.41), channel_id=1, replica_groups=mesh['row'=8,'col'=4] {'row','col'}, use_global_device_ids=true, to_apply=%region_9.0 | all-reduce | flops 2 | bytes 16 | tf_op jit(solution)/shard_map/psum | solution.py:60
  205.6 1.3 collective-permute-start.16
  208.8 5.0 %collective-permute-start.23 = (f32[258,1]{1,0:T(8,128)S(1)}, f32[258,1]{1,0:T(8,128)S(1)}, u32[]{:S(2)}, u32[]{:S(2)}) collective-permute-start(f32[258,1]{1,0:T(8,128)S(1)} %get-tuple-element.44), channel_id=1, source_target_pairs={{0,1},{1,2},{2,3},{4,5},{5,6},{6,7},{8,9},{9,10},{10,11},{12,13},{... | collective-permute-start | bytes 3104 | tf_op jit(solution)/shard_map/ppermute | solution.py:19
  214.0 1.3 collective-permute-start.18
  215.3 5.4 %collective-permute-start.19 = (f32[258,1]{1,0:T(8,128)S(1)}, f32[258,1]{1,0:T(8,128)S(1)}, u32[]{:S(2)}, u32[]{:S(2)}) collective-permute-start(f32[258,1]{1,0:T(8,128)S(1)} %get-tuple-element.42), channel_id=1, source_target_pairs={{0,1},{1,2},{2,3},{4,5},{5,6},{6,7},{8,9},{9,10},{10,11},{12,13},{... | collective-permute-start | bytes 3104 | tf_op jit(solution)/shard_map/ppermute | solution.py:19
  220.8 2.5 collective-permute-done.18
  223.6 3.4 fusion.71
  227.0 44.8 %all-reduce.2 = (f32[]{:T(128)}, f32[]{:T(128)}) all-reduce(f32[]{:T(128)} %get-tuple-element.5, f32[]{:T(128)} %get-tuple-element.4), channel_id=1, replica_groups=mesh['row'=8,'col'=4] {'row','col'}, use_global_device_ids=true, to_apply=%region_13.0 | all-reduce | flops 2 | bytes 16 | tf_op jit(solution)/shard_map/psum | solution.py:60
  274.5 1.3 collective-permute-start.24
  275.9 2.3 collective-permute-done.24
  279.6 4.8 %collective-permute-start.27 = (f32[258,1]{1,0:T(8,128)S(1)}, f32[258,1]{1,0:T(8,128)S(1)}, u32[]{:S(2)}, u32[]{:S(2)}) collective-permute-start(f32[258,1]{1,0:T(8,128)S(1)} %get-tuple-element.40), channel_id=1, source_target_pairs={{0,1},{1,2},{2,3},{4,5},{5,6},{6,7},{8,9},{9,10},{10,11},{12,13},{... | collective-permute-start | bytes 3104 | tf_op jit(solution)/shard_map/ppermute | solution.py:19
  285.5 1.5 collective-permute-done.27
  287.0 3.9 multiply_reduce_fusion.2
  290.9 44.6 %all-reduce.1 = (f32[]{:T(128)}, f32[]{:T(128)}) all-reduce(f32[]{:T(128)} %get-tuple-element.8, f32[]{:T(128)} %get-tuple-element.7), channel_id=1, replica_groups=mesh['row'=8,'col'=4] {'row','col'}, use_global_device_ids=true, to_apply=%region_17.0 | all-reduce | flops 2 | bytes 16 | tf_op jit(solution)/shard_map/psum | solution.py:60
  339.9 1.8 multiply_reduce_fusion.1
  343.1 1.4 collective-permute-start.28
  344.5 2.4 collective-permute-done.28
  348.3 4.8 %collective-permute-start.31 = (f32[258,1]{1,0:T(8,128)S(1)}, f32[258,1]{1,0:T(8,128)S(1)}, u32[]{:S(2)}, u32[]{:S(2)}) collective-permute-start(f32[258,1]{1,0:T(8,128)S(1)} %get-tuple-element.38), channel_id=1, source_target_pairs={{0,1},{1,2},{2,3},{4,5},{5,6},{6,7},{8,9},{9,10},{10,11},{12,13},{... | collective-permute-start | bytes 3104 | tf_op jit(solution)/shard_map/ppermute | solution.py:19
  354.2 1.5 collective-permute-done.31
  355.7 3.1 fusion.5
  358.8 44.5 %all-reduce = (f32[]{:T(128)}, f32[]{:T(128)}, f32[]{:T(128)}, f32[]{:T(128)}) all-reduce(f32[]{:T(128)} %get-tuple-element.27, f32[]{:T(128)} %fusion.5, f32[]{:T(128)} %get-tuple-element.6, f32[]{:T(128)} %get-tuple-element.3), channel_id=1, replica_groups=mesh['row'=8,'col'=4] {'row','col'}, use_global_device_ids=true, to_apply=%region_21.0 | all-reduce | flops 4 | bytes 32 | tf_op jit(solution)/shard_map/psum | solution.py:60
  (81 shorter events, 16.7 us)
Async XLA Ops:
  2.2 10.2 %collective-permute-start.5 = (f32[1,512]{1,0:T(1,128)S(1)}, f32[1,512]{1,0:T(1,128)S(1)}, u32[]{:S(2)}, u32[]{:S(2)}) collective-permute-start(f32[1,512]{1,0:T(1,128)S(1)} %get-tuple-element.67), channel_id=1, source_target_pairs={{0,4},{4,8},{8,12},{12,16},{16,20},{20,24},{24,28},{1,5},{5,9},{9,... | collective-permute-start | bytes 6152 | tf_op jit(solution)/shard_map/ppermute | solution.py:19
  4.6 7.8 %collective-permute-start.4 = (f32[1,512]{1,0:T(1,128)S(1)}, f32[1,512]{1,0:T(1,128)S(1)}, u32[]{:S(2)}, u32[]{:S(2)}) collective-permute-start(f32[1,512]{1,0:T(1,128)S(1)} %get-tuple-element.68), channel_id=1, source_target_pairs={{4,0},{8,4},{12,8},{16,12},{20,16},{24,20},{28,24},{5,1},{9,5},{13... | collective-permute-start | bytes 6152 | tf_op jit(solution)/shard_map/ppermute | solution.py:21
  5.9 12.5 %collective-permute-start.1 = (f32[1,512]{1,0:T(1,128)S(1)}, f32[1,512]{1,0:T(1,128)S(1)}, u32[]{:S(2)}, u32[]{:S(2)}) collective-permute-start(f32[1,512]{1,0:T(1,128)S(1)} %get-tuple-element.65), channel_id=1, source_target_pairs={{0,4},{4,8},{8,12},{12,16},{16,20},{20,24},{24,28},{1,5},{5,9},{9,... | collective-permute-start | bytes 6152 | tf_op jit(solution)/shard_map/ppermute | solution.py:19
  11.1 7.3 %collective-permute-start = (f32[1,512]{1,0:T(1,128)S(1)}, f32[1,512]{1,0:T(1,128)S(1)}, u32[]{:S(2)}, u32[]{:S(2)}) collective-permute-start(f32[1,512]{1,0:T(1,128)S(1)} %get-tuple-element.66), channel_id=1, source_target_pairs={{4,0},{8,4},{12,8},{16,12},{20,16},{24,20},{28,24},{5,1},{9,5},{13... | collective-permute-start | bytes 6152 | tf_op jit(solution)/shard_map/ppermute | solution.py:21
  12.5 12.2 %collective-permute-start.6 = (f32[258,1]{1,0:T(8,128)S(1)}, f32[258,1]{1,0:T(8,128)S(1)}, u32[]{:S(2)}, u32[]{:S(2)}) collective-permute-start(f32[258,1]{1,0:T(8,128)S(1)} %get-tuple-element.51), channel_id=1, source_target_pairs={{1,0},{2,1},{3,2},{5,4},{6,5},{7,6},{9,8},{10,9},{11,10},{13,12},{... | collective-permute-start | bytes 3104 | tf_op jit(solution)/shard_map/ppermute | solution.py:21
  13.8 11.0 %collective-permute-start.7 = (f32[258,1]{1,0:T(8,128)S(1)}, f32[258,1]{1,0:T(8,128)S(1)}, u32[]{:S(2)}, u32[]{:S(2)}) collective-permute-start(f32[258,1]{1,0:T(8,128)S(1)} %get-tuple-element.52), channel_id=1, source_target_pairs={{0,1},{1,2},{2,3},{4,5},{5,6},{6,7},{8,9},{9,10},{10,11},{12,13},{... | collective-permute-start | bytes 3104 | tf_op jit(solution)/shard_map/ppermute | solution.py:19
  18.4 138.7 %copy-start.4 = (f32[1,512]{1,0:T(1,128)}, f32[1,512]{1,0:T(1,128)S(1)}, u32[]{:S(2)}) copy-start(f32[1,512]{1,0:T(1,128)S(1)} %collective-permute-done) | copy-start | bytes 6148
  18.6 8.7 %collective-permute-start.2 = (f32[258,1]{1,0:T(8,128)S(1)}, f32[258,1]{1,0:T(8,128)S(1)}, u32[]{:S(2)}, u32[]{:S(2)}) collective-permute-start(f32[258,1]{1,0:T(8,128)S(1)} %get-tuple-element.49), channel_id=1, source_target_pairs={{1,0},{2,1},{3,2},{5,4},{6,5},{7,6},{9,8},{10,9},{11,10},{13,12},{... | collective-permute-start | bytes 3104 | tf_op jit(solution)/shard_map/ppermute | solution.py:21
  19.9 8.0 %collective-permute-start.3 = (f32[258,1]{1,0:T(8,128)S(1)}, f32[258,1]{1,0:T(8,128)S(1)}, u32[]{:S(2)}, u32[]{:S(2)}) collective-permute-start(f32[258,1]{1,0:T(8,128)S(1)} %get-tuple-element.50), channel_id=1, source_target_pairs={{0,1},{1,2},{2,3},{4,5},{5,6},{6,7},{8,9},{9,10},{10,11},{12,13},{... | collective-permute-start | bytes 3104 | tf_op jit(solution)/shard_map/ppermute | solution.py:19
  75.2 2.6 collective-permute-start.9
  76.5 4.7 %collective-permute-start.8 = (f32[1,512]{1,0:T(1,128)S(1)}, f32[1,512]{1,0:T(1,128)S(1)}, u32[]{:S(2)}, u32[]{:S(2)}) collective-permute-start(f32[1,512]{1,0:T(1,128)S(1)} %get-tuple-element.64), channel_id=1, source_target_pairs={{4,0},{8,4},{12,8},{16,12},{20,16},{24,20},{28,24},{5,1},{9,5},{13... | collective-permute-start | bytes 6152 | tf_op jit(solution)/shard_map/ppermute | solution.py:21
  81.4 7.2 %collective-permute-start.10 = (f32[258,1]{1,0:T(8,128)S(1)}, f32[258,1]{1,0:T(8,128)S(1)}, u32[]{:S(2)}, u32[]{:S(2)}) collective-permute-start(f32[258,1]{1,0:T(8,128)S(1)} %get-tuple-element.47), channel_id=1, source_target_pairs={{1,0},{2,1},{3,2},{5,4},{6,5},{7,6},{9,8},{10,9},{11,10},{13,12},{... | collective-permute-start | bytes 3104 | tf_op jit(solution)/shard_map/ppermute | solution.py:21
  82.7 7.4 %collective-permute-start.11 = (f32[258,1]{1,0:T(8,128)S(1)}, f32[258,1]{1,0:T(8,128)S(1)}, u32[]{:S(2)}, u32[]{:S(2)}) collective-permute-start(f32[258,1]{1,0:T(8,128)S(1)} %get-tuple-element.48), channel_id=1, source_target_pairs={{0,1},{1,2},{2,3},{4,5},{5,6},{6,7},{8,9},{9,10},{10,11},{12,13},{... | collective-permute-start | bytes 3104 | tf_op jit(solution)/shard_map/ppermute | solution.py:19
  140.9 10.9 %copy-start.1 = (f32[256,512]{1,0:T(8,128)S(1)}, f32[256,512]{1,0:T(8,128)}, u32[]{:S(2)}) copy-start(f32[256,512]{1,0:T(8,128)} %param.7) | copy-start | bytes 1572868
  141.0 2.7 collective-permute-start.13
  142.4 3.2 collective-permute-start.12
  145.7 11.4 %collective-permute-start.14 = (f32[258,1]{1,0:T(8,128)S(1)}, f32[258,1]{1,0:T(8,128)S(1)}, u32[]{:S(2)}, u32[]{:S(2)}) collective-permute-start(f32[258,1]{1,0:T(8,128)S(1)} %get-tuple-element.45), channel_id=1, source_target_pairs={{1,0},{2,1},{3,2},{5,4},{6,5},{7,6},{9,8},{10,9},{11,10},{13,12},{... | collective-permute-start | bytes 3104 | tf_op jit(solution)/shard_map/ppermute | solution.py:21
  147.0 10.1 %collective-permute-start.15 = (f32[258,1]{1,0:T(8,128)S(1)}, f32[258,1]{1,0:T(8,128)S(1)}, u32[]{:S(2)}, u32[]{:S(2)}) collective-permute-start(f32[258,1]{1,0:T(8,128)S(1)} %get-tuple-element.46), channel_id=1, source_target_pairs={{0,1},{1,2},{2,3},{4,5},{5,6},{6,7},{8,9},{9,10},{10,11},{12,13},{... | collective-permute-start | bytes 3104 | tf_op jit(solution)/shard_map/ppermute | solution.py:19
  151.9 55.0 %collective-permute-start.21 = (f32[1,512]{1,0:T(1,128)S(1)}, f32[1,512]{1,0:T(1,128)S(1)}, u32[]{:S(2)}, u32[]{:S(2)}) collective-permute-start(f32[1,512]{1,0:T(1,128)S(1)} %get-tuple-element.59), channel_id=1, source_target_pairs={{0,4},{4,8},{8,12},{12,16},{16,20},{20,24},{24,28},{1,5},{5,9},{9,... | collective-permute-start | bytes 6152 | tf_op jit(solution)/shard_map/ppermute | solution.py:19
  155.8 51.1 %collective-permute-start.20 = (f32[1,512]{1,0:T(1,128)S(1)}, f32[1,512]{1,0:T(1,128)S(1)}, u32[]{:S(2)}, u32[]{:S(2)}) collective-permute-start(f32[1,512]{1,0:T(1,128)S(1)} %get-tuple-element.60), channel_id=1, source_target_pairs={{4,0},{8,4},{12,8},{16,12},{20,16},{24,20},{28,24},{5,1},{9,5},{13... | collective-permute-start | bytes 6152 | tf_op jit(solution)/shard_map/ppermute | solution.py:21
  204.2 151.4 %copy-start = (f32[256,512]{1,0:T(8,128)}, f32[256,512]{1,0:T(8,128)S(1)}, u32[]{:S(2)}) copy-start(f32[256,512]{1,0:T(8,128)S(1)} %multiply_add_fusion.1) | copy-start | bytes 1572868
  204.3 9.6 %collective-permute-start.17 = (f32[1,512]{1,0:T(1,128)S(1)}, f32[1,512]{1,0:T(1,128)S(1)}, u32[]{:S(2)}, u32[]{:S(2)}) collective-permute-start(f32[1,512]{1,0:T(1,128)S(1)} %get-tuple-element.57), channel_id=1, source_target_pairs={{0,4},{4,8},{8,12},{12,16},{16,20},{20,24},{24,28},{1,5},{5,9},{9,... | collective-permute-start | bytes 6152 | tf_op jit(solution)/shard_map/ppermute | solution.py:19
  205.6 8.3 %collective-permute-start.16 = (f32[1,512]{1,0:T(1,128)S(1)}, f32[1,512]{1,0:T(1,128)S(1)}, u32[]{:S(2)}, u32[]{:S(2)}) collective-permute-start(f32[1,512]{1,0:T(1,128)S(1)} %get-tuple-element.58), channel_id=1, source_target_pairs={{4,0},{8,4},{12,8},{16,12},{20,16},{24,20},{28,24},{5,1},{9,5},{13... | collective-permute-start | bytes 6152 | tf_op jit(solution)/shard_map/ppermute | solution.py:21
  206.9 0.6 copy-start.11
  206.9 0.6 copy-start.13
  207.5 13.3 %collective-permute-start.22 = (f32[258,1]{1,0:T(8,128)S(1)}, f32[258,1]{1,0:T(8,128)S(1)}, u32[]{:S(2)}, u32[]{:S(2)}) collective-permute-start(f32[258,1]{1,0:T(8,128)S(1)} %get-tuple-element.43), channel_id=1, source_target_pairs={{1,0},{2,1},{3,2},{5,4},{6,5},{7,6},{9,8},{10,9},{11,10},{13,12},{... | collective-permute-start | bytes 3104 | tf_op jit(solution)/shard_map/ppermute | solution.py:21
  208.8 12.0 %collective-permute-start.23 = (f32[258,1]{1,0:T(8,128)S(1)}, f32[258,1]{1,0:T(8,128)S(1)}, u32[]{:S(2)}, u32[]{:S(2)}) collective-permute-start(f32[258,1]{1,0:T(8,128)S(1)} %get-tuple-element.44), channel_id=1, source_target_pairs={{0,1},{1,2},{2,3},{4,5},{5,6},{6,7},{8,9},{9,10},{10,11},{12,13},{... | collective-permute-start | bytes 3104 | tf_op jit(solution)/shard_map/ppermute | solution.py:19
  213.8 73.1 %copy-start.7 = (f32[1,512]{1,0:T(1,128)}, f32[1,512]{1,0:T(1,128)S(1)}, u32[]{:S(2)}) copy-start(f32[1,512]{1,0:T(1,128)S(1)} %collective-permute-done.17) | copy-start | bytes 6148
  213.9 73.1 %copy-start.9 = (f32[1,512]{1,0:T(1,128)}, f32[1,512]{1,0:T(1,128)S(1)}, u32[]{:S(2)}) copy-start(f32[1,512]{1,0:T(1,128)S(1)} %collective-permute-done.16) | copy-start | bytes 6148
  213.9 9.7 %copy-start.12 = (f32[1,512]{1,0:T(1,128)S(1)}, f32[1,512]{1,0:T(1,128)}, u32[]{:S(2)}) copy-start(f32[1,512]{1,0:T(1,128)} %copy-done.11) | copy-start | bytes 6148
  213.9 9.7 %copy-start.14 = (f32[1,512]{1,0:T(1,128)S(1)}, f32[1,512]{1,0:T(1,128)}, u32[]{:S(2)}) copy-start(f32[1,512]{1,0:T(1,128)} %copy-done.13) | copy-start | bytes 6148
  214.0 9.6 %copy-start.5 = (f32[1,512]{1,0:T(1,128)S(1)}, f32[1,512]{1,0:T(1,128)}, u32[]{:S(2)}) copy-start(f32[1,512]{1,0:T(1,128)} %copy-done.4) | copy-start | bytes 6148
  214.0 9.2 %collective-permute-start.18 = (f32[258,1]{1,0:T(8,128)S(1)}, f32[258,1]{1,0:T(8,128)S(1)}, u32[]{:S(2)}, u32[]{:S(2)}) collective-permute-start(f32[258,1]{1,0:T(8,128)S(1)} %get-tuple-element.41), channel_id=1, source_target_pairs={{1,0},{2,1},{3,2},{5,4},{6,5},{7,6},{9,8},{10,9},{11,10},{13,12},{... | collective-permute-start | bytes 3104 | tf_op jit(solution)/shard_map/ppermute | solution.py:21
  215.3 8.2 %collective-permute-start.19 = (f32[258,1]{1,0:T(8,128)S(1)}, f32[258,1]{1,0:T(8,128)S(1)}, u32[]{:S(2)}, u32[]{:S(2)}) collective-permute-start(f32[258,1]{1,0:T(8,128)S(1)} %get-tuple-element.42), channel_id=1, source_target_pairs={{0,1},{1,2},{2,3},{4,5},{5,6},{6,7},{8,9},{9,10},{10,11},{12,13},{... | collective-permute-start | bytes 3104 | tf_op jit(solution)/shard_map/ppermute | solution.py:19
  223.6 63.4 %copy-start.2 = (f32[258,1]{1,0:T(8,128)}, f32[258,1]{1,0:T(8,128)S(1)}, u32[]{:S(2)}) copy-start(f32[258,1]{1,0:T(8,128)S(1)} %collective-permute-done.19) | copy-start | bytes 3100
  273.2 2.6 collective-permute-start.25
  274.5 3.7 collective-permute-start.24
  278.3 7.2 %collective-permute-start.26 = (f32[258,1]{1,0:T(8,128)S(1)}, f32[258,1]{1,0:T(8,128)S(1)}, u32[]{:S(2)}, u32[]{:S(2)}) collective-permute-start(f32[258,1]{1,0:T(8,128)S(1)} %get-tuple-element.39), channel_id=1, source_target_pairs={{1,0},{2,1},{3,2},{5,4},{6,5},{7,6},{9,8},{10,9},{11,10},{13,12},{... | collective-permute-start | bytes 3104 | tf_op jit(solution)/shard_map/ppermute | solution.py:21
  279.6 7.4 %collective-permute-start.27 = (f32[258,1]{1,0:T(8,128)S(1)}, f32[258,1]{1,0:T(8,128)S(1)}, u32[]{:S(2)}, u32[]{:S(2)}) collective-permute-start(f32[258,1]{1,0:T(8,128)S(1)} %get-tuple-element.40), channel_id=1, source_target_pairs={{0,1},{1,2},{2,3},{4,5},{5,6},{6,7},{8,9},{9,10},{10,11},{12,13},{... | collective-permute-start | bytes 3104 | tf_op jit(solution)/shard_map/ppermute | solution.py:19
  341.8 2.7 collective-permute-start.29
  343.1 12.6 %copy-start.3 = (f32[258,1]{1,0:T(8,128)S(1)}, f32[258,1]{1,0:T(8,128)}, u32[]{:S(2)}) copy-start(f32[258,1]{1,0:T(8,128)} %copy-done.2) | copy-start | bytes 3100
  343.1 3.8 collective-permute-start.28
  346.9 8.8 %copy-start.8 = (f32[1,512]{1,0:T(1,128)S(1)}, f32[1,512]{1,0:T(1,128)}, u32[]{:S(2)}) copy-start(f32[1,512]{1,0:T(1,128)} %copy-done.7) | copy-start | bytes 6148
  346.9 8.8 %copy-start.10 = (f32[1,512]{1,0:T(1,128)S(1)}, f32[1,512]{1,0:T(1,128)}, u32[]{:S(2)}) copy-start(f32[1,512]{1,0:T(1,128)} %copy-done.9) | copy-start | bytes 6148
  347.0 8.7 %copy-start.6 = (f32[1,512]{1,0:T(1,128)S(1)}, f32[1,512]{1,0:T(1,128)}, u32[]{:S(2)}) copy-start(f32[1,512]{1,0:T(1,128)} %copy-done.4) | copy-start | bytes 6148
  347.0 7.2 %collective-permute-start.30 = (f32[258,1]{1,0:T(8,128)S(1)}, f32[258,1]{1,0:T(8,128)S(1)}, u32[]{:S(2)}, u32[]{:S(2)}) collective-permute-start(f32[258,1]{1,0:T(8,128)S(1)} %get-tuple-element.37), channel_id=1, source_target_pairs={{1,0},{2,1},{3,2},{5,4},{6,5},{7,6},{9,8},{10,9},{11,10},{13,12},{... | collective-permute-start | bytes 3104 | tf_op jit(solution)/shard_map/ppermute | solution.py:21
  348.3 7.4 %collective-permute-start.31 = (f32[258,1]{1,0:T(8,128)S(1)}, f32[258,1]{1,0:T(8,128)S(1)}, u32[]{:S(2)}, u32[]{:S(2)}) collective-permute-start(f32[258,1]{1,0:T(8,128)S(1)} %get-tuple-element.38), channel_id=1, source_target_pairs={{0,1},{1,2},{2,3},{4,5},{5,6},{6,7},{8,9},{9,10},{10,11},{12,13},{... | collective-permute-start | bytes 3104 | tf_op jit(solution)/shard_map/ppermute | solution.py:19
where the time goes:
time: 413 us; the launch traced here: 411 us
  blocking collectives  264 us (64%)
  starting transfers between devices  78.2 us (19%)
  waiting for transfers between devices  23.6 us (6%)
  between operations  22.8 us (6%)
  other arithmetic  21 us (5%)
    psum x6, blocking collectives, products(): lax.psum((jnp.sum(residual * residual), jnp.sum(residual * applied)), ('r...  264 us
    ppermute x16, starting transfers between devices, padded_2(): lax.ppermute(tail, axis, [(i, (i + 1) % count) for i in range(ends)])  57.4 us
    ppermute x16, starting transfers between devices, padded_2(): lax.ppermute(head, axis, [((i + 1) % count, i) for i in range(ends)])  20.8 us
    ppermute x16, waiting for transfers between devices, padded_2(): lax.ppermute(head, axis, [((i + 1) % count, i) for i in range(ends)])  18.1 us
    reduce_sum x5, other arithmetic, products(): jnp.sum(residual * applied)  11.2 us
  transfers between devices with their start and end apart: 32, of which 14 were waited for; matrix products, arithmetic and copies ran while one was open for 0% of the time, Pallas kernels for 0%

commit v1 on v0

--- a/solution.py
+++ b/solution.py
@@ -57,7 +57,9 @@
 
 
 def products(residual, applied):
-    return lax.psum((jnp.sum(residual * residual), jnp.sum(residual * applied)), ("row", "col"))
+    return lax.psum(
+        lax.psum((jnp.sum(residual * residual), jnp.sum(residual * applied)), "col"), "row"
+    )
 
 
 def conjugate(coeffs, forcing):

time: 413 us -> 342 us (0.83)
  blocking collectives: 264 us -> 196 us
    psum x6 -> x13, blocking collectives: 264 us -> 196 us  [the longest x6 86.1 us: products(): lax.psum(lax.psum((jnp.sum(residual * residual), jnp.sum(residual * appli...]
  transfers between devices with their start and end apart: 32 -> 32, of which waited for: 14 -> 12; matrix products, arithmetic and copies ran while one was open for 0% -> 1% of each run, Pallas kernels for 0% -> 0%
where the time goes in v1:
time: 342 us; the launch traced here: 340 us
  blocking collectives  196 us (57%)
  starting transfers between devices  78.7 us (23%)
  between operations  23.2 us (7%)
  other arithmetic  21.9 us (6%)
  waiting for transfers between devices  20.2 us (6%)
    psum x6, blocking collectives, products(): lax.psum(lax.psum((jnp.sum(residual * residual), jnp.sum(residual * appli...  86.1 us
    psum x6, blocking collectives, products(): lax.psum((jnp.sum(residual * residual), jnp.sum(residual * applied)), 'col')  70 us
    ppermute x16, starting transfers between devices, padded_2(): lax.ppermute(tail, axis, [(i, (i + 1) % count) for i in range(ends)])  57.9 us
    psum x1, blocking collectives, body(): totals = lax.psum((weighted, weight_total), ('row', 'col'))  39.9 us
    ppermute x16, starting transfers between devices, padded_2(): lax.ppermute(head, axis, [((i + 1) % count, i) for i in range(ends)])  20.8 us
    ppermute x16, waiting for transfers between devices, padded_2(): lax.ppermute(head, axis, [((i + 1) % count, i) for i in range(ends)])  15.6 us
    reduce_sum x5, other arithmetic, products(): jnp.sum(residual * applied)  12.1 us
  transfers between devices with their start and end apart: 32, of which 12 were waited for; matrix products, arithmetic and copies ran while one was open for 1% of the time, Pallas kernels for 0%

profile of v1, /device:TPU:0, one launch (start us, length us, event | category | flops | bytes accessed | tf_op | source)
XLA Modules:
  0.0 340.5 jit_solution(263929621522827390)
XLA Ops:
  0.6 1.5 broadcast_add_fusion
  2.2 2.4 collective-permute-start.5
  5.9 5.2 %collective-permute-start.1 = (f32[1,512]{1,0:T(1,128)S(1)}, f32[1,512]{1,0:T(1,128)S(1)}, u32[]{:S(2)}, u32[]{:S(2)}) collective-permute-start(f32[1,512]{1,0:T(1,128)S(1)} %get-tuple-element.77), channel_id=1, source_target_pairs={{0,4},{4,8},{8,12},{12,16},{16,20},{20,24},{24,28},{1,5},{5,9},{9,... | collective-permute-start | bytes 6152 | tf_op jit(solution)/shard_map/ppermute | solution.py:19
  13.8 4.6 %collective-permute-start.7 = (f32[258,1]{1,0:T(8,128)S(1)}, f32[258,1]{1,0:T(8,128)S(1)}, u32[]{:S(2)}, u32[]{:S(2)}) collective-permute-start(f32[258,1]{1,0:T(8,128)S(1)} %get-tuple-element.64), channel_id=1, source_target_pairs={{0,1},{1,2},{2,3},{4,5},{5,6},{6,7},{8,9},{9,10},{10,11},{12,13},{... | collective-permute-start | bytes 3104 | tf_op jit(solution)/shard_map/ppermute | solution.py:19
  19.9 4.9 %collective-permute-start.3 = (f32[258,1]{1,0:T(8,128)S(1)}, f32[258,1]{1,0:T(8,128)S(1)}, u32[]{:S(2)}, u32[]{:S(2)}) collective-permute-start(f32[258,1]{1,0:T(8,128)S(1)} %get-tuple-element.62), channel_id=1, source_target_pairs={{0,1},{1,2},{2,3},{4,5},{5,6},{6,7},{8,9},{9,10},{10,11},{12,13},{... | collective-permute-start | bytes 3104 | tf_op jit(solution)/shard_map/ppermute | solution.py:19
  24.8 2.5 collective-permute-done.2
  27.9 1.4 multiply_reduce_fusion.9
  29.3 12.4 %all-reduce.12 = (f32[]{:T(128)}, f32[]{:T(128)}) all-reduce(f32[]{:T(128)} %get-tuple-element.12, f32[]{:T(128)} %get-tuple-element.11), channel_id=1, replica_groups=mesh['row'=8,'col'=4] {'col'}, use_global_device_ids=true, to_apply=%region_1.0 | all-reduce | flops 2 | bytes 16 | tf_op jit(solution)/shard_map/psum | solution.py:61
  41.7 14.9 %all-reduce.6 = (f32[]{:T(128)}, f32[]{:T(128)}) all-reduce(f32[]{:T(128)} %get-tuple-element.37, f32[]{:T(128)} %get-tuple-element.38), channel_id=1, replica_groups=mesh['row'=8,'col'=4] {'row'}, use_global_device_ids=true, to_apply=%region_2.0 | all-reduce | flops 2 | bytes 16 | tf_op jit(solution)/shard_map/psum | solution.py:60
  58.1 2.2 collective-permute-start.9
  61.6 1.7 collective-permute-done.8
  64.8 4.6 %collective-permute-start.11 = (f32[258,1]{1,0:T(8,128)S(1)}, f32[258,1]{1,0:T(8,128)S(1)}, u32[]{:S(2)}, u32[]{:S(2)}) collective-permute-start(f32[258,1]{1,0:T(8,128)S(1)} %get-tuple-element.60), channel_id=1, source_target_pairs={{0,1},{1,2},{2,3},{4,5},{5,6},{6,7},{8,9},{9,10},{10,11},{12,13},{... | collective-permute-start | bytes 3104 | tf_op jit(solution)/shard_map/ppermute | solution.py:19
  69.4 1.4 collective-permute-done.10
  70.8 1.7 collective-permute-done.11
  72.5 1.4 multiply_reduce_fusion.7
  74.0 12.2 %all-reduce.11 = (f32[]{:T(128)}, f32[]{:T(128)}) all-reduce(f32[]{:T(128)} %get-tuple-element.10, f32[]{:T(128)} %get-tuple-element.9), channel_id=1, replica_groups=mesh['row'=8,'col'=4] {'col'}, use_global_device_ids=true, to_apply=%region_7.0 | all-reduce | flops 2 | bytes 16 | tf_op jit(solution)/shard_map/psum | solution.py:61
  86.2 14.2 %all-reduce.5 = (f32[]{:T(128)}, f32[]{:T(128)}) all-reduce(f32[]{:T(128)} %get-tuple-element.35, f32[]{:T(128)} %get-tuple-element.36), channel_id=1, replica_groups=mesh['row'=8,'col'=4] {'row'}, use_global_device_ids=true, to_apply=%region_8.0 | all-reduce | flops 2 | bytes 16 | tf_op jit(solution)/shard_map/psum | solution.py:60
  105.7 1.9 collective-permute-start.13
  109.0 1.7 collective-permute-done.12
  112.1 4.6 %collective-permute-start.15 = (f32[258,1]{1,0:T(8,128)S(1)}, f32[258,1]{1,0:T(8,128)S(1)}, u32[]{:S(2)}, u32[]{:S(2)}) collective-permute-start(f32[258,1]{1,0:T(8,128)S(1)} %get-tuple-element.58), channel_id=1, source_target_pairs={{0,1},{1,2},{2,3},{4,5},{5,6},{6,7},{8,9},{9,10},{10,11},{12,13},{... | collective-permute-start | bytes 3104 | tf_op jit(solution)/shard_map/ppermute | solution.py:19
  116.7 3.2 collective-permute-start.21
  121.3 1.4 fusion.41
  122.7 10.3 %all-reduce.10 = (f32[]{:T(128)}, f32[]{:T(128)}) all-reduce(f32[]{:T(128)} %get-tuple-element.43, f32[]{:T(128)} %fusion.41), channel_id=1, replica_groups=mesh['row'=8,'col'=4] {'col'}, use_global_device_ids=true, to_apply=%region_13.0 | all-reduce | flops 2 | bytes 16 | tf_op jit(solution)/shard_map/psum | solution.py:61
  133.0 14.2 %all-reduce.4 = (f32[]{:T(128)}, f32[]{:T(128)}) all-reduce(f32[]{:T(128)} %get-tuple-element.33, f32[]{:T(128)} %get-tuple-element.34), channel_id=1, replica_groups=mesh['row'=8,'col'=4] {'row'}, use_global_device_ids=true, to_apply=%region_14.0 | all-reduce | flops 2 | bytes 16 | tf_op jit(solution)/shard_map/psum | solution.py:60
  151.3 1.8 collective-permute-start.17
  156.3 4.6 %collective-permute-start.23 = (f32[258,1]{1,0:T(8,128)S(1)}, f32[258,1]{1,0:T(8,128)S(1)}, u32[]{:S(2)}, u32[]{:S(2)}) collective-permute-start(f32[258,1]{1,0:T(8,128)S(1)} %get-tuple-element.56), channel_id=1, source_target_pairs={{0,1},{1,2},{2,3},{4,5},{5,6},{6,7},{8,9},{9,10},{10,11},{12,13},{... | collective-permute-start | bytes 3104 | tf_op jit(solution)/shard_map/ppermute | solution.py:19
  162.3 4.7 %collective-permute-start.19 = (f32[258,1]{1,0:T(8,128)S(1)}, f32[258,1]{1,0:T(8,128)S(1)}, u32[]{:S(2)}, u32[]{:S(2)}) collective-permute-start(f32[258,1]{1,0:T(8,128)S(1)} %get-tuple-element.54), channel_id=1, source_target_pairs={{0,1},{1,2},{2,3},{4,5},{5,6},{6,7},{8,9},{9,10},{10,11},{12,13},{... | collective-permute-start | bytes 3104 | tf_op jit(solution)/shard_map/ppermute | solution.py:19
  167.1 3.1 collective-permute-done.18
  170.6 3.4 fusion.71
  174.0 12.4 %all-reduce.9 = (f32[]{:T(128)}, f32[]{:T(128)}) all-reduce(f32[]{:T(128)} %get-tuple-element.5, f32[]{:T(128)} %get-tuple-element.4), channel_id=1, replica_groups=mesh['row'=8,'col'=4] {'col'}, use_global_device_ids=true, to_apply=%region_19.0 | all-reduce | flops 2 | bytes 16 | tf_op jit(solution)/shard_map/psum | solution.py:61
  186.4 14.3 %all-reduce.3 = (f32[]{:T(128)}, f32[]{:T(128)}) all-reduce(f32[]{:T(128)} %get-tuple-element.31, f32[]{:T(128)} %get-tuple-element.32), channel_id=1, replica_groups=mesh['row'=8,'col'=4] {'row'}, use_global_device_ids=true, to_apply=%region_20.0 | all-reduce | flops 2 | bytes 16 | tf_op jit(solution)/shard_map/psum | solution.py:60
  202.1 1.8 collective-permute-start.25
  205.2 1.7 collective-permute-done.24
  208.4 4.6 %collective-permute-start.27 = (f32[258,1]{1,0:T(8,128)S(1)}, f32[258,1]{1,0:T(8,128)S(1)}, u32[]{:S(2)}, u32[]{:S(2)}) collective-permute-start(f32[258,1]{1,0:T(8,128)S(1)} %get-tuple-element.52), channel_id=1, source_target_pairs={{0,1},{1,2},{2,3},{4,5},{5,6},{6,7},{8,9},{9,10},{10,11},{12,13},{... | collective-permute-start | bytes 3104 | tf_op jit(solution)/shard_map/ppermute | solution.py:19
  212.9 1.6 collective-permute-done.26
  214.5 1.7 collective-permute-done.27
  216.3 3.9 %multiply_reduce_fusion.2 = (f32[]{:T(128)}, f32[]{:T(128)}, f32[256,512]{1,0:T(8,128)}) fusion(f32[256,512]{1,0:T(8,128)S(1)} %multiply_subtract_fusion.1, f32[1,512]{1,0:T(1,128)S(1)} %collective-permute-done.24, f32[1,512]{1,0:T(1,128)S(1)} %collective-permute-done.25, f32[258,1]{1,0:T(8,128)S(1)} %collective-permute-done.27, ...), kind=kLoop, calls=%fused_computation.138 | loop fusion | flops 7602174 | bytes 2115640 | tf_op jit(solution)/shard_map/reduce_sum | solution.py:61
  220.2 11.2 %all-reduce.8 = (f32[]{:T(128)}, f32[]{:T(128)}) all-reduce(f32[]{:T(128)} %get-tuple-element.8, f32[]{:T(128)} %get-tuple-element.7), channel_id=1, replica_groups=mesh['row'=8,'col'=4] {'col'}, use_global_device_ids=true, to_apply=%region_25.0 | all-reduce | flops 2 | bytes 16 | tf_op jit(solution)/shard_map/psum | solution.py:61
  231.4 14.3 %all-reduce.2 = (f32[]{:T(128)}, f32[]{:T(128)}) all-reduce(f32[]{:T(128)} %get-tuple-element.29, f32[]{:T(128)} %get-tuple-element.30), channel_id=1, replica_groups=mesh['row'=8,'col'=4] {'row'}, use_global_device_ids=true, to_apply=%region_26.0 | all-reduce | flops 2 | bytes 16 | tf_op jit(solution)/shard_map/psum | solution.py:60
  250.2 1.8 multiply_reduce_fusion.1
  252.0 1.8 collective-permute-start.29
  253.8 1.4 collective-permute-start.28
  255.2 1.7 collective-permute-done.28
  258.4 5.2 %collective-permute-start.31 = (f32[258,1]{1,0:T(8,128)S(1)}, f32[258,1]{1,0:T(8,128)}, u32[]{:S(2)}, u32[]{:S(2)}) collective-permute-start(f32[258,1]{1,0:T(8,128)S(1)} %get-tuple-element.50), channel_id=1, source_target_pairs={{0,1},{1,2},{2,3},{4,5},{5,6},{6,7},{8,9},{9,10},{10,11},{12,13},{... | collective-permute-start | bytes 3104 | tf_op jit(solution)/shard_map/ppermute | solution.py:19
  263.6 39.9 %all-reduce = (f32[]{:T(128)}, f32[]{:T(128)}) all-reduce(f32[]{:T(128)} %get-tuple-element.6, f32[]{:T(128)} %get-tuple-element.3), channel_id=1, replica_groups=mesh['row'=8,'col'=4] {'row','col'}, use_global_device_ids=true, to_apply=%region_37.0 | all-reduce | flops 2 | bytes 16 | tf_op jit(solution)/shard_map/psum | solution.py:103
  304.9 4.0 %fusion.5 = f32[]{:T(128)} fusion(f32[256,512]{1,0:T(8,128)S(1)} %get-tuple-element.40, f32[258,1]{1,0:T(8,128)} %collective-permute-done.31, f32[1,512]{1,0:T(1,128)S(1)} %collective-permute-done.28, f32[1,512]{1,0:T(1,128)S(1)} %collective-permute-done.29, f32[258,1]{1,0:T(8,128)} %collective-permute-done.30, f32[256,512]{1,0:T(8,128)S(1)} %get-tuple-element.47, ...), kind=kLoop, calls=%fused_computation.6 | loop fusion | flops 7340031 | bytes 1591348 | tf_op jit(solution)/shard_map/reduce_sum | solution.py:61
  308.9 11.4 %all-reduce.7 = (f32[]{:T(128)}, f32[]{:T(128)}) all-reduce(f32[]{:T(128)} %get-tuple-element.39, f32[]{:T(128)} %fusion.5), channel_id=1, replica_groups=mesh['row'=8,'col'=4] {'col'}, use_global_device_ids=true, to_apply=%region_31.0 | all-reduce | flops 2 | bytes 16 | tf_op jit(solution)/shard_map/psum | solution.py:61
  320.3 14.2 %all-reduce.1 = (f32[]{:T(128)}, f32[]{:T(128)}) all-reduce(f32[]{:T(128)} %get-tuple-element.27, f32[]{:T(128)} %get-tuple-element.28), channel_id=1, replica_groups=mesh['row'=8,'col'=4] {'row'}, use_global_device_ids=true, to_apply=%region_32.0 | all-reduce | flops 2 | bytes 16 | tf_op jit(solution)/shard_map/psum | solution.py:60
  (88 shorter events, 24.0 us)
Async XLA Ops:
  2.2 10.2 %collective-permute-start.5 = (f32[1,512]{1,0:T(1,128)S(1)}, f32[1,512]{1,0:T(1,128)S(1)}, u32[]{:S(2)}, u32[]{:S(2)}) collective-permute-start(f32[1,512]{1,0:T(1,128)S(1)} %get-tuple-element.79), channel_id=1, source_target_pairs={{0,4},{4,8},{8,12},{12,16},{16,20},{20,24},{24,28},{1,5},{5,9},{9,... | collective-permute-start | bytes 6152 | tf_op jit(solution)/shard_map/ppermute | solution.py:19
  4.6 7.8 %collective-permute-start.4 = (f32[1,512]{1,0:T(1,128)S(1)}, f32[1,512]{1,0:T(1,128)S(1)}, u32[]{:S(2)}, u32[]{:S(2)}) collective-permute-start(f32[1,512]{1,0:T(1,128)S(1)} %get-tuple-element.80), channel_id=1, source_target_pairs={{4,0},{8,4},{12,8},{16,12},{20,16},{24,20},{28,24},{5,1},{9,5},{13... | collective-permute-start | bytes 6152 | tf_op jit(solution)/shard_map/ppermute | solution.py:21
  5.9 12.5 %collective-permute-start.1 = (f32[1,512]{1,0:T(1,128)S(1)}, f32[1,512]{1,0:T(1,128)S(1)}, u32[]{:S(2)}, u32[]{:S(2)}) collective-permute-start(f32[1,512]{1,0:T(1,128)S(1)} %get-tuple-element.77), channel_id=1, source_target_pairs={{0,4},{4,8},{8,12},{12,16},{16,20},{20,24},{24,28},{1,5},{5,9},{9,... | collective-permute-start | bytes 6152 | tf_op jit(solution)/shard_map/ppermute | solution.py:19
  11.1 7.3 %collective-permute-start = (f32[1,512]{1,0:T(1,128)S(1)}, f32[1,512]{1,0:T(1,128)S(1)}, u32[]{:S(2)}, u32[]{:S(2)}) collective-permute-start(f32[1,512]{1,0:T(1,128)S(1)} %get-tuple-element.78), channel_id=1, source_target_pairs={{4,0},{8,4},{12,8},{16,12},{20,16},{24,20},{28,24},{5,1},{9,5},{13... | collective-permute-start | bytes 6152 | tf_op jit(solution)/shard_map/ppermute | solution.py:21
  12.5 12.2 %collective-permute-start.6 = (f32[258,1]{1,0:T(8,128)S(1)}, f32[258,1]{1,0:T(8,128)S(1)}, u32[]{:S(2)}, u32[]{:S(2)}) collective-permute-start(f32[258,1]{1,0:T(8,128)S(1)} %get-tuple-element.63), channel_id=1, source_target_pairs={{1,0},{2,1},{3,2},{5,4},{6,5},{7,6},{9,8},{10,9},{11,10},{13,12},{... | collective-permute-start | bytes 3104 | tf_op jit(solution)/shard_map/ppermute | solution.py:21
  13.8 11.0 %collective-permute-start.7 = (f32[258,1]{1,0:T(8,128)S(1)}, f32[258,1]{1,0:T(8,128)S(1)}, u32[]{:S(2)}, u32[]{:S(2)}) collective-permute-start(f32[258,1]{1,0:T(8,128)S(1)} %get-tuple-element.64), channel_id=1, source_target_pairs={{0,1},{1,2},{2,3},{4,5},{5,6},{6,7},{8,9},{9,10},{10,11},{12,13},{... | collective-permute-start | bytes 3104 | tf_op jit(solution)/shard_map/ppermute | solution.py:19
  18.4 102.8 %copy-start.4 = (f32[1,512]{1,0:T(1,128)}, f32[1,512]{1,0:T(1,128)S(1)}, u32[]{:S(2)}) copy-start(f32[1,512]{1,0:T(1,128)S(1)} %collective-permute-done) | copy-start | bytes 6148
  18.6 8.7 %collective-permute-start.2 = (f32[258,1]{1,0:T(8,128)S(1)}, f32[258,1]{1,0:T(8,128)S(1)}, u32[]{:S(2)}, u32[]{:S(2)}) collective-permute-start(f32[258,1]{1,0:T(8,128)S(1)} %get-tuple-element.61), channel_id=1, source_target_pairs={{1,0},{2,1},{3,2},{5,4},{6,5},{7,6},{9,8},{10,9},{11,10},{13,12},{... | collective-permute-start | bytes 3104 | tf_op jit(solution)/shard_map/ppermute | solution.py:21
  19.9 8.0 %collective-permute-start.3 = (f32[258,1]{1,0:T(8,128)S(1)}, f32[258,1]{1,0:T(8,128)S(1)}, u32[]{:S(2)}, u32[]{:S(2)}) collective-permute-start(f32[258,1]{1,0:T(8,128)S(1)} %get-tuple-element.62), channel_id=1, source_target_pairs={{0,1},{1,2},{2,3},{4,5},{5,6},{6,7},{8,9},{9,10},{10,11},{12,13},{... | collective-permute-start | bytes 3104 | tf_op jit(solution)/shard_map/ppermute | solution.py:19
  58.1 3.6 %collective-permute-start.9 = (f32[1,512]{1,0:T(1,128)S(1)}, f32[1,512]{1,0:T(1,128)S(1)}, u32[]{:S(2)}, u32[]{:S(2)}) collective-permute-start(f32[1,512]{1,0:T(1,128)S(1)} %get-tuple-element.75), channel_id=1, source_target_pairs={{0,4},{4,8},{8,12},{12,16},{16,20},{20,24},{24,28},{1,5},{5,9},{9,... | collective-permute-start | bytes 6152 | tf_op jit(solution)/shard_map/ppermute | solution.py:19
  60.3 3.1 collective-permute-start.8
  63.5 7.3 %collective-permute-start.10 = (f32[258,1]{1,0:T(8,128)S(1)}, f32[258,1]{1,0:T(8,128)S(1)}, u32[]{:S(2)}, u32[]{:S(2)}) collective-permute-start(f32[258,1]{1,0:T(8,128)S(1)} %get-tuple-element.59), channel_id=1, source_target_pairs={{1,0},{2,1},{3,2},{5,4},{6,5},{7,6},{9,8},{10,9},{11,10},{13,12},{... | collective-permute-start | bytes 3104 | tf_op jit(solution)/shard_map/ppermute | solution.py:21
  64.8 7.8 %collective-permute-start.11 = (f32[258,1]{1,0:T(8,128)S(1)}, f32[258,1]{1,0:T(8,128)S(1)}, u32[]{:S(2)}, u32[]{:S(2)}) collective-permute-start(f32[258,1]{1,0:T(8,128)S(1)} %get-tuple-element.60), channel_id=1, source_target_pairs={{0,1},{1,2},{2,3},{4,5},{5,6},{6,7},{8,9},{9,10},{10,11},{12,13},{... | collective-permute-start | bytes 3104 | tf_op jit(solution)/shard_map/ppermute | solution.py:19
  105.7 11.0 %copy-start.1 = (f32[256,512]{1,0:T(8,128)S(1)}, f32[256,512]{1,0:T(8,128)}, u32[]{:S(2)}) copy-start(f32[256,512]{1,0:T(8,128)} %param.7) | copy-start | bytes 1572868
  105.7 3.2 collective-permute-start.13
  107.7 3.1 collective-permute-start.12
  110.8 10.4 %collective-permute-start.14 = (f32[258,1]{1,0:T(8,128)S(1)}, f32[258,1]{1,0:T(8,128)S(1)}, u32[]{:S(2)}, u32[]{:S(2)}) collective-permute-start(f32[258,1]{1,0:T(8,128)S(1)} %get-tuple-element.57), channel_id=1, source_target_pairs={{1,0},{2,1},{3,2},{5,4},{6,5},{7,6},{9,8},{10,9},{11,10},{13,12},{... | collective-permute-start | bytes 3104 | tf_op jit(solution)/shard_map/ppermute | solution.py:21
  112.1 9.1 %collective-permute-start.15 = (f32[258,1]{1,0:T(8,128)S(1)}, f32[258,1]{1,0:T(8,128)S(1)}, u32[]{:S(2)}, u32[]{:S(2)}) collective-permute-start(f32[258,1]{1,0:T(8,128)S(1)} %get-tuple-element.58), channel_id=1, source_target_pairs={{0,1},{1,2},{2,3},{4,5},{5,6},{6,7},{8,9},{9,10},{10,11},{12,13},{... | collective-permute-start | bytes 3104 | tf_op jit(solution)/shard_map/ppermute | solution.py:19
  116.7 37.6 %collective-permute-start.21 = (f32[1,512]{1,0:T(1,128)S(1)}, f32[1,512]{1,0:T(1,128)S(1)}, u32[]{:S(2)}, u32[]{:S(2)}) collective-permute-start(f32[1,512]{1,0:T(1,128)S(1)} %get-tuple-element.71), channel_id=1, source_target_pairs={{0,4},{4,8},{8,12},{12,16},{16,20},{20,24},{24,28},{1,5},{5,9},{9,... | collective-permute-start | bytes 6152 | tf_op jit(solution)/shard_map/ppermute | solution.py:19
  119.9 34.4 %collective-permute-start.20 = (f32[1,512]{1,0:T(1,128)S(1)}, f32[1,512]{1,0:T(1,128)S(1)}, u32[]{:S(2)}, u32[]{:S(2)}) collective-permute-start(f32[1,512]{1,0:T(1,128)S(1)} %get-tuple-element.72), channel_id=1, source_target_pairs={{4,0},{8,4},{12,8},{16,12},{20,16},{24,20},{28,24},{5,1},{9,5},{13... | collective-permute-start | bytes 6152 | tf_op jit(solution)/shard_map/ppermute | solution.py:21
  151.3 153.6 %copy-start = (f32[256,512]{1,0:T(8,128)}, f32[256,512]{1,0:T(8,128)S(1)}, u32[]{:S(2)}) copy-start(f32[256,512]{1,0:T(8,128)S(1)} %multiply_add_fusion.1) | copy-start | bytes 1572868
  151.3 9.5 %collective-permute-start.17 = (f32[1,512]{1,0:T(1,128)S(1)}, f32[1,512]{1,0:T(1,128)S(1)}, u32[]{:S(2)}, u32[]{:S(2)}) collective-permute-start(f32[1,512]{1,0:T(1,128)S(1)} %get-tuple-element.69), channel_id=1, source_target_pairs={{0,4},{4,8},{8,12},{12,16},{16,20},{20,24},{24,28},{1,5},{5,9},{9,... | collective-permute-start | bytes 6152 | tf_op jit(solution)/shard_map/ppermute | solution.py:19
  153.1 7.8 %collective-permute-start.16 = (f32[1,512]{1,0:T(1,128)S(1)}, f32[1,512]{1,0:T(1,128)S(1)}, u32[]{:S(2)}, u32[]{:S(2)}) collective-permute-start(f32[1,512]{1,0:T(1,128)S(1)} %get-tuple-element.70), channel_id=1, source_target_pairs={{4,0},{8,4},{12,8},{16,12},{20,16},{24,20},{28,24},{5,1},{9,5},{13... | collective-permute-start | bytes 6152 | tf_op jit(solution)/shard_map/ppermute | solution.py:21
  154.4 0.6 copy-start.11
  154.4 0.6 copy-start.13
  155.0 12.1 %collective-permute-start.22 = (f32[258,1]{1,0:T(8,128)S(1)}, f32[258,1]{1,0:T(8,128)S(1)}, u32[]{:S(2)}, u32[]{:S(2)}) collective-permute-start(f32[258,1]{1,0:T(8,128)S(1)} %get-tuple-element.55), channel_id=1, source_target_pairs={{1,0},{2,1},{3,2},{5,4},{6,5},{7,6},{9,8},{10,9},{11,10},{13,12},{... | collective-permute-start | bytes 3104 | tf_op jit(solution)/shard_map/ppermute | solution.py:21
  156.3 10.8 %collective-permute-start.23 = (f32[258,1]{1,0:T(8,128)S(1)}, f32[258,1]{1,0:T(8,128)S(1)}, u32[]{:S(2)}, u32[]{:S(2)}) collective-permute-start(f32[258,1]{1,0:T(8,128)S(1)} %get-tuple-element.56), channel_id=1, source_target_pairs={{0,1},{1,2},{2,3},{4,5},{5,6},{6,7},{8,9},{9,10},{10,11},{12,13},{... | collective-permute-start | bytes 3104 | tf_op jit(solution)/shard_map/ppermute | solution.py:19
  160.8 55.4 %copy-start.7 = (f32[1,512]{1,0:T(1,128)}, f32[1,512]{1,0:T(1,128)S(1)}, u32[]{:S(2)}) copy-start(f32[1,512]{1,0:T(1,128)S(1)} %collective-permute-done.17) | copy-start | bytes 6148
  160.9 55.4 %copy-start.9 = (f32[1,512]{1,0:T(1,128)}, f32[1,512]{1,0:T(1,128)S(1)}, u32[]{:S(2)}) copy-start(f32[1,512]{1,0:T(1,128)S(1)} %collective-permute-done.16) | copy-start | bytes 6148
  160.9 9.7 %copy-start.12 = (f32[1,512]{1,0:T(1,128)S(1)}, f32[1,512]{1,0:T(1,128)}, u32[]{:S(2)}) copy-start(f32[1,512]{1,0:T(1,128)} %copy-done.11) | copy-start | bytes 6148
  160.9 9.7 %copy-start.14 = (f32[1,512]{1,0:T(1,128)S(1)}, f32[1,512]{1,0:T(1,128)}, u32[]{:S(2)}) copy-start(f32[1,512]{1,0:T(1,128)} %copy-done.13) | copy-start | bytes 6148
  161.0 9.6 %copy-start.5 = (f32[1,512]{1,0:T(1,128)S(1)}, f32[1,512]{1,0:T(1,128)}, u32[]{:S(2)}) copy-start(f32[1,512]{1,0:T(1,128)} %copy-done.4) | copy-start | bytes 6148
  161.0 9.2 %collective-permute-start.18 = (f32[258,1]{1,0:T(8,128)S(1)}, f32[258,1]{1,0:T(8,128)S(1)}, u32[]{:S(2)}, u32[]{:S(2)}) collective-permute-start(f32[258,1]{1,0:T(8,128)S(1)} %get-tuple-element.53), channel_id=1, source_target_pairs={{1,0},{2,1},{3,2},{5,4},{6,5},{7,6},{9,8},{10,9},{11,10},{13,12},{... | collective-permute-start | bytes 3104 | tf_op jit(solution)/shard_map/ppermute | solution.py:21
  162.3 8.3 %collective-permute-start.19 = (f32[258,1]{1,0:T(8,128)S(1)}, f32[258,1]{1,0:T(8,128)S(1)}, u32[]{:S(2)}, u32[]{:S(2)}) collective-permute-start(f32[258,1]{1,0:T(8,128)S(1)} %get-tuple-element.54), channel_id=1, source_target_pairs={{0,1},{1,2},{2,3},{4,5},{5,6},{6,7},{8,9},{9,10},{10,11},{12,13},{... | collective-permute-start | bytes 3104 | tf_op jit(solution)/shard_map/ppermute | solution.py:19
  170.6 45.7 %copy-start.2 = (f32[258,1]{1,0:T(8,128)}, f32[258,1]{1,0:T(8,128)S(1)}, u32[]{:S(2)}) copy-start(f32[258,1]{1,0:T(8,128)S(1)} %collective-permute-done.19) | copy-start | bytes 3100
  202.1 3.1 collective-permute-start.25
  203.9 3.1 collective-permute-start.24
  207.1 7.5 %collective-permute-start.26 = (f32[258,1]{1,0:T(8,128)S(1)}, f32[258,1]{1,0:T(8,128)S(1)}, u32[]{:S(2)}, u32[]{:S(2)}) collective-permute-start(f32[258,1]{1,0:T(8,128)S(1)} %get-tuple-element.51), channel_id=1, source_target_pairs={{1,0},{2,1},{3,2},{5,4},{6,5},{7,6},{9,8},{10,9},{11,10},{13,12},{... | collective-permute-start | bytes 3104 | tf_op jit(solution)/shard_map/ppermute | solution.py:21
  208.4 7.9 %collective-permute-start.27 = (f32[258,1]{1,0:T(8,128)S(1)}, f32[258,1]{1,0:T(8,128)S(1)}, u32[]{:S(2)}, u32[]{:S(2)}) collective-permute-start(f32[258,1]{1,0:T(8,128)S(1)} %get-tuple-element.52), channel_id=1, source_target_pairs={{0,1},{1,2},{2,3},{4,5},{5,6},{6,7},{8,9},{9,10},{10,11},{12,13},{... | collective-permute-start | bytes 3104 | tf_op jit(solution)/shard_map/ppermute | solution.py:19
  252.0 3.2 collective-permute-start.29
  253.8 51.1 %copy-start.3 = (f32[258,1]{1,0:T(8,128)S(1)}, f32[258,1]{1,0:T(8,128)}, u32[]{:S(2)}) copy-start(f32[258,1]{1,0:T(8,128)} %copy-done.2) | copy-start | bytes 3100
  253.8 3.2 collective-permute-start.28
  257.0 47.9 %copy-start.10 = (f32[1,512]{1,0:T(1,128)S(1)}, f32[1,512]{1,0:T(1,128)}, u32[]{:S(2)}) copy-start(f32[1,512]{1,0:T(1,128)} %copy-done.9) | copy-start | bytes 6148
  257.1 47.7 %collective-permute-start.30 = (f32[258,1]{1,0:T(8,128)S(1)}, f32[258,1]{1,0:T(8,128)}, u32[]{:S(2)}, u32[]{:S(2)}) collective-permute-start(f32[258,1]{1,0:T(8,128)S(1)} %get-tuple-element.49), channel_id=1, source_target_pairs={{1,0},{2,1},{3,2},{5,4},{6,5},{7,6},{9,8},{10,9},{11,10},{13,12},{... | collective-permute-start | bytes 3104 | tf_op jit(solution)/shard_map/ppermute | solution.py:21
  258.4 46.4 %collective-permute-start.31 = (f32[258,1]{1,0:T(8,128)S(1)}, f32[258,1]{1,0:T(8,128)}, u32[]{:S(2)}, u32[]{:S(2)}) collective-permute-start(f32[258,1]{1,0:T(8,128)S(1)} %get-tuple-element.50), channel_id=1, source_target_pairs={{0,1},{1,2},{2,3},{4,5},{5,6},{6,7},{8,9},{9,10},{10,11},{12,13},{... | collective-permute-start | bytes 3104 | tf_op jit(solution)/shard_map/ppermute | solution.py:19
  303.5 1.4 copy-start.8
  303.5 1.4 copy-start.6
